TPU v7x, 512 devices: a whole 4x4x16 slice. The times are simulated.
512 devices in a mesh: din: 16 (over z), dout: 32 (over y, x, core).
Axes of the slice: x: 4, y: 4, z: 16, core: 2. Of those that a mesh axis runs over, the one named last changes fastest.
Arguments:
- inputs: bfloat16 [2048, 8192], P('dout', 'din'), may hold values from -6 to 6
- cotangent: bfloat16 [2048, 28672], P('din', 'dout'), may hold values from -6 to 6
- codes: int32 [2, 1024, 28672], P(None, 'din', 'dout'), may hold values from 0 to 255
- codebooks: float32 [2, 256, 8], replicated, may hold values from -6 to 6
- scales: float32 [28672], P('dout'), may hold values from 0.5 to 2
- book_mean: float32 [2, 256, 8], replicated, may hold values from -3 to 3
- book_var: float32 [2, 256, 8], replicated, may hold values from 0.1 to 1
- scale_mean: float32 [28672], P('dout'), may hold values from -3 to 3
- scale_var: float32 [28672], P('dout'), may hold values from 0.1 to 1
Outputs:
- grad_input: bfloat16 [2048, 8192], P('dout', 'din')
- book_grad: float32 [2, 256, 8], replicated
- new_books: float32 [2, 256, 8], replicated
- new_book_mean: float32 [2, 256, 8], replicated
- new_book_var: float32 [2, 256, 8], replicated
- new_scales: float32 [28672], P('dout')
- new_scale_mean: float32 [28672], P('dout')
- new_scale_var: float32 [28672], P('dout')
Inputs may be any that keep to these rules, and one draw needn't show every extreme that they name: codes[b, g, o] names the entry of codebook b used for input features 8 * g to 8 * g + 7 of output o.
All inputs are finite; a program needn't handle non-finite values.
Results may differ from a plain program's by a relative error of at most 0.0057.
Values may be sent and summed in bfloat16 or wider, within the bound.
A program may use at most 64 MiB of HBM per device.

v0:
```python
import math

import jax
import jax.numpy as jnp
from jax import lax
from jax.sharding import PartitionSpec as P

DIN = 8192
DOUT = 28672
KCODE = 256
BOOKS = 2
GROUP = 8
TOKENS = 2048


beta_one = 0.9
beta_two = 0.999
adam_rate = 0.01
adam_eps = 1e-08
corr_one = 1.0 - 0.9**10
corr_two = 1.0 - 0.999**10


def adam_step(param, mean_old, var_old, gradient):
    mean_new = beta_one * mean_old + (1.0 - beta_one) * gradient
    var_new = beta_two * var_old + (1.0 - beta_two) * gradient * gradient
    update = mean_new / corr_one / (jnp.sqrt(var_new / corr_two) + adam_eps)
    return (param - adam_rate * update, mean_new, var_new)


def local(inputs, cotangent, codes, codebooks, scales, book_mean, book_var, scale_mean, scale_var):
    norm_factor = 1.0 / (2.0 * DOUT) ** 0.5
    loss_scale = (TOKENS * DIN / 4096.0) ** 0.5
    coef = scales * norm_factor
    groups_dev = codes.shape[1]
    outs_dev = codes.shape[2]
    gy_full = lax.all_gather(cotangent, "din", axis=0, tiled=True)
    x_full = lax.all_gather(inputs, "dout", axis=0, tiled=True)
    grad_w = lax.dot_general(
        x_full, gy_full, (((0,), (0,)), ((), ())), preferred_element_type=jnp.float32
    )
    grad_three = grad_w.reshape(groups_dev, GROUP, outs_dev)
    scaled = (grad_three * coef).astype(jnp.bfloat16)
    books_bf = codebooks.astype(jnp.bfloat16)
    code_iota = lax.iota(jnp.int32, KCODE)[:, None, None]
    scale_local = jnp.zeros((outs_dev,), jnp.float32)
    grad_local = jnp.zeros((BOOKS, KCODE, GROUP), jnp.float32)
    scale_total = scale_local
    grad_total = grad_local
    block_groups = math.gcd(4, groups_dev)

    def decode_block(turn_index, state_tuple):
        weight_tile, scale_run, grad_run = state_tuple
        local_first = turn_index * block_groups
        global_first = 0 + local_first
        code_block = lax.dynamic_slice_in_dim(codes, global_first, block_groups, 1)
        grad_block = lax.dynamic_slice_in_dim(grad_three, global_first, block_groups, 0)
        scaled_block = lax.dynamic_slice_in_dim(scaled, global_first, block_groups, 0)
        decoded = jnp.zeros((block_groups, GROUP, outs_dev), jnp.float32)
        book_terms = []
        for which_book in range(BOOKS):
            onehot = (code_block[which_book][None] == code_iota).astype(jnp.bfloat16)
            decoded = decoded + jnp.einsum(
                "kj,kgo->gjo", books_bf[which_book], onehot, preferred_element_type=jnp.float32
            )
            book_terms.append(
                jnp.einsum("kgo,gjo->kj", onehot, scaled_block, preferred_element_type=jnp.float32)
            )
        weight_new = (decoded * coef).astype(jnp.bfloat16)
        weight_tile = lax.dynamic_update_slice_in_dim(weight_tile, weight_new, local_first, 0)
        scale_run = scale_run + jnp.sum(decoded * grad_block, axis=(0, 1))
        grad_run = grad_run + jnp.stack(book_terms)
        return (weight_tile, scale_run, grad_run)

    start_state = (jnp.zeros((groups_dev, GROUP, outs_dev), jnp.bfloat16), scale_total, grad_total)
    weight_tile, scale_total, grad_total = lax.fori_loop(
        0, groups_dev // block_groups, decode_block, start_state
    )
    weight_flat = weight_tile.reshape(groups_dev * GROUP, outs_dev)
    grad_rows = lax.psum_scatter(
        lax.dot_general(
            gy_full, weight_flat, (((1,), (1,)), ((), ())), preferred_element_type=jnp.float32
        ),
        "dout",
        scatter_dimension=0,
        tiled=True,
    )
    grad_input = grad_rows.astype(jnp.bfloat16)
    scale_sums = lax.psum(scale_total, "din")
    grad_sums = lax.psum(grad_total, ("din", "dout"))
    book_grad = grad_sums / loss_scale
    scale_grad = scale_sums * norm_factor / loss_scale
    new_books, new_book_mean, new_book_var = adam_step(codebooks, book_mean, book_var, book_grad)
    new_scales, new_scale_mean, new_scale_var = adam_step(scales, scale_mean, scale_var, scale_grad)
    return (
        grad_input,
        book_grad,
        new_books,
        new_book_mean,
        new_book_var,
        new_scales,
        new_scale_mean,
        new_scale_var,
    )


def solution(mesh):
    in_specs = (
        P("dout", "din"),
        P("din", "dout"),
        P(None, "din", "dout"),
        P(),
        P("dout"),
        P(),
        P(),
        P("dout"),
        P("dout"),
    )
    out_specs = (P("dout", "din"), P(), P(), P(), P(), P("dout"), P("dout"), P("dout"))
    return jax.shard_map(local, mesh=mesh, in_specs=in_specs, out_specs=out_specs, check_vma=False)
```

profile of v0, /device:TPU:1, one launch (start us, length us, event | category | flops | bytes accessed | tf_op | source)
XLA Modules:
  0.0 393.1 jit_solution(6351678988470089029)
XLA Ops:
  10.1 65.6 %all-gather.3.cloned.1.call-done = bf16[2048,512]{1,0:T(8,128)(2,1)} async-done(((bf16[64,512]{1,0:T(8,128)(2,1)}), bf16[2048,512]{1,0:T(8,128)(2,1)}) %all-gather.3.cloned.1.call-update) | async-done | bytes 2097168 | tf_op jit(solution)/shard_map/all_gather | solution.py:38
  75.7 68.8 %all-gather.5.cloned.1.call-done = bf16[2048,896]{1,0:T(8,128)(2,1)} async-done(((bf16[128,896]{1,0:T(8,128)(2,1)}), bf16[2048,896]{1,0:T(8,128)(2,1)}) %all-gather.5.cloned.1.call-update) | async-done | bytes 3670032 | tf_op jit(solution)/shard_map/all_gather | solution.py:37
  144.5 6.0 %multiply_convert_fusion.1 = (bf16[64,8,896]{2,1,0:T(8,128)(2,1)}, f32[64,8,896]{2,1,0:T(8,128)S(1)}) fusion(f32[896]{0:T(1024)S(1)} %broadcast_multiply_fusion.1, bf16[2048,512]{1,0:T(8,128)(2,1)} %all-gather.3.cloned.1.call-done, bf16[2048,896]{1,0:T(8,128)(2,1)} %all-gather.5.cloned.1.call-done), kind=kOutput, calls=%fused_computation.31 | convolution fusion | flops 1879965696 | bytes 8523264 | tf_op jit(solution)/shard_map/dot_general | solution.py:39
  150.5 82.2 %while.19 = (s32[]{:T(128)}, bf16[64,8,896]{2,1,0:T(8,128)(2,1)S(1)}, f32[896]{0:T(1024)S(1)}, f32[2,256,8]{1,2,0:T(8,128)S(1)}, s32[2,64,896]{2,1,0:T(8,128)}, ...) while((s32[]{:T(128)}, ...), condition=%wide.region_2.0_spmd.clone.clone, body=%wide.region_0.0_spmd.clone.clone.sunk | while | flops 62546824 | bytes 952554 | solution.py:76
  152.8 1.5 fusion.39
  157.9 1.5 fusion.39
  163.1 1.5 fusion.39
  168.2 1.5 fusion.39
  173.4 1.5 fusion.39
  178.5 1.5 fusion.39
  183.6 1.5 fusion.39
  188.8 1.5 fusion.39
  193.9 1.5 fusion.39
  199.1 1.5 fusion.39
  204.2 1.5 fusion.39
  209.3 1.5 fusion.39
  214.5 1.5 fusion.39
  219.6 1.5 fusion.39
  224.8 1.5 fusion.39
  229.9 1.5 fusion.39
  232.8 6.4 %convolution_bitcast_fusion = f32[2048,512]{0,1:T(8,128)} fusion(bf16[2048,896]{1,0:T(8,128)(2,1)} %all-gather.5.cloned.1.call-done, bf16[64,8,896]{2,1,0:T(8,128)(2,1)S(1)} %get-tuple-element.182), kind=kOutput, calls=%fused_computation.30 | convolution fusion | flops 1879048192 | bytes 8781824 | tf_op jit(solution)/shard_map/dot_general | solution.py:81
  239.1 5.4 %copy.20 = f32[2048,512]{1,0:T(8,128)} copy(f32[2048,512]{0,1:T(8,128)} %convolution_bitcast_fusion) | data formatting | bytes 8388608
  244.6 22.2 %psum.15 = f32[896]{0:T(1024)S(1)} all-reduce(f32[896]{0:T(1024)S(1)} %get-tuple-element.184), channel_id=1, replica_groups=mesh['din'=16,'dout'=32] {'din'}, use_global_device_ids=true, to_apply=%region_5.0 | all-reduce | flops 896 | bytes 7168 | tf_op jit(solution)/shard_map/psum | solution.py:89
  266.8 116.8 %psum.14 = f32[2,256,8]{1,2,0:T(8,128)S(1)} all-reduce(f32[2,256,8]{1,2,0:T(8,128)S(1)} %get-tuple-element.183), channel_id=1, replica_groups=mesh['din'=16,'dout'=32] {'din','dout'}, use_global_device_ids=true, to_apply=%region_4.0 | all-reduce | flops 4096 | bytes 32768 | tf_op jit(solution)/shard_map/psum | solution.py:90
  (140 shorter events, 64.0 us)
Async XLA Ops:
  7.2 68.5 %all-gather.3.cloned.1.call-start = ((), (), s32[]{:S(2)}) async-start(), calls=%async_computation.1 | async-start | bytes 2162688 | tf_op jit(solution)/shard_map/all_gather | solution.py:38
  7.9 136.6 %all-gather.5.cloned.1.call-start = ((), (), s32[]{:S(2)}) async-start(), calls=%async_computation.2 | async-start | bytes 3899392 | tf_op jit(solution)/shard_map/all_gather | solution.py:37
  8.6 376.2 %reduce-scatter.4.cloned.1.call-start = ((), (), s32[]{:S(2)}) async-start(), calls=%async_computation.3 | async-start | bytes 4325376
  244.5 139.1 %copy-start.1 = (f32[896]{0:T(1024)S(1)}, f32[896]{0:T(1024)}, u32[]{:S(2)}) copy-start(f32[896]{0:T(1024)} %param.15) | copy-start | bytes 10756
  244.5 139.1 %copy-start.4 = (f32[896]{0:T(1024)S(1)}, f32[896]{0:T(1024)}, u32[]{:S(2)}) copy-start(f32[896]{0:T(1024)} %param.18) | copy-start | bytes 10756
  244.5 139.1 %copy-start.5 = (f32[896]{0:T(1024)S(1)}, f32[896]{0:T(1024)}, u32[]{:S(2)}) copy-start(f32[896]{0:T(1024)} %param.19) | copy-start | bytes 10756
  244.5 139.7 %copy-start = (f32[2,256,8]{1,2,0:T(8,128)S(1)}, f32[2,256,8]{1,2,0:T(8,128)}, u32[]{:S(2)}) copy-start(f32[2,256,8]{1,2,0:T(8,128)} %param.14) | copy-start | bytes 49156
  244.5 139.7 %copy-start.2 = (f32[2,256,8]{1,2,0:T(8,128)S(1)}, f32[2,256,8]{1,2,0:T(8,128)}, u32[]{:S(2)}) copy-start(f32[2,256,8]{1,2,0:T(8,128)} %param.16) | copy-start | bytes 49156
  244.5 139.7 %copy-start.3 = (f32[2,256,8]{1,2,0:T(8,128)S(1)}, f32[2,256,8]{1,2,0:T(8,128)}, u32[]{:S(2)}) copy-start(f32[2,256,8]{1,2,0:T(8,128)} %param.17) | copy-start | bytes 49156
Sparse Core Ops, SparseCore 0:
  11.1 64.5 all-gather.2
  77.8 66.6 all-gather.4
  244.7 110.0 reduce-scatter.3
where the time goes:
time: 396 us; the launch traced here: 393 us
  blocking collectives  139 us (35%)
  waiting for transfers between devices  136 us (34%)
  matrix products  80.8 us (20%)
  local copies, waits for them, and re-layouts  19.7 us (5%)
  between operations  13.8 us (3%)
    psum x1, blocking collectives, local(): grad_sums = lax.psum(grad_total, ('din', 'dout'))  117 us
    all_gather x1, waiting for transfers between devices, local(): gy_full = lax.all_gather(cotangent, 'din', axis=0, tiled=True)  68.8 us
    all_gather x1, waiting for transfers between devices, local(): x_full = lax.all_gather(inputs, 'dout', axis=0, tiled=True)  65.6 us
    dot_general x32, matrix products, decode_block(): jnp.einsum('kgo,gjo->kj', onehot, scaled_block, preferred_element_type=jn...  47.3 us
    psum x1, blocking collectives, local(): scale_sums = lax.psum(scale_total, 'din')  22.2 us
    dot_general x32, matrix products, decode_block(): jnp.einsum('kj,kgo->gjo', books_bf[which_book], onehot, preferred_element...  21.2 us
    eq x16, local copies, waits for them, and re-layouts, decode_block(): onehot = (code_block[which_book][None] == code_iota).astype(jnp.bfloat16)  12.5 us
  transfers between devices with their start and end apart: 3, of which 2 were waited for; matrix products, arithmetic and copies ran while one was open for 1% of the time, Pallas kernels for 0%

commit v1 on v0

v1 whole, which is shorter than its diff:
```python
import functools

import jax
import jax.numpy as jnp
from jax import lax
from jax.experimental import pallas as pl
from jax.experimental.pallas import tpu as pltpu
from jax.sharding import PartitionSpec as P

DIN = 8192
DOUT = 28672
KCODE = 256
BOOKS = 2
GROUP = 8
TOKENS = 2048

beta_one = 0.9
beta_two = 0.999
adam_rate = 0.01
adam_eps = 1e-08
corr_one = 1.0 - 0.9**10
corr_two = 1.0 - 0.999**10

LANES = 128
LOW = 8
HIGH = KCODE // LOW


def adam_step(param, mean_old, var_old, gradient):
    mean_new = beta_one * mean_old + (1.0 - beta_one) * gradient
    var_new = beta_two * var_old + (1.0 - beta_two) * gradient * gradient
    update = mean_new / corr_one / (jnp.sqrt(var_new / corr_two) + adam_eps)
    return (param - adam_rate * update, mean_new, var_new)


def kernel(
    nz, nd, x_hbm, gy_hbm, codes, table, coef, gx_out, book_out, scale_out,
    gyf, xf, xt, wts, dec, gw, gkeep, gst, gpr, rss, rsr, hloc, hpair, hsum, hplane, hz, hfin, sown, sz,
    loc_sem, gy_send, gy_recv, x_send, x_recv, p_send, p_recv, r_send, r_recv,
    hp_send, hp_recv, hx_send, hx_recv, hz_send, hz_recv, hf_send, hf_recv, s_send, s_recv,
):
    chips = nd // 2
    half = nz // 2
    nc = gyf.shape[0]
    cl = (nc + 1) // 2
    rows = gy_hbm.shape[0]
    xrows = x_hbm.shape[0]
    feats = x_hbm.shape[1]
    groups = codes.shape[1]
    iz = lax.axis_index("din")
    jd = lax.axis_index("dout")
    chip = jd // 2
    core = jd % 2
    mate = jd + 1 - 2 * core
    right = lax.rem(iz + 1, nz)
    left = lax.rem(iz + nz - 1, nz)
    f32 = jnp.float32
    bf16 = jnp.bfloat16

    def remote(src, dst, ssem, rsem, din=None, dout=None):
        where = {}
        if din is not None:
            where["din"] = din
        if dout is not None:
            where["dout"] = dout
        return pltpu.make_async_remote_copy(
            src_ref=src, dst_ref=dst, send_sem=ssem, recv_sem=rsem,
            device_id=where, device_id_type=pl.DeviceIdType.MESH,
        )

    def rows_of(block):
        return pl.ds(pl.multiple_of(block * rows, rows), rows)

    for c in range(nc):
        pltpu.make_async_copy(
            gy_hbm.at[:, pl.ds(c * LANES, LANES)], gyf.at[c, rows_of(iz)], loc_sem.at[c]
        ).start()
    pltpu.make_async_copy(x_hbm, xf.at[jd], loc_sem.at[nc]).start()

    barrier = pltpu.get_barrier_semaphore()
    for k in range(1, nz):
        pl.semaphore_signal(barrier, 1, device_id={"din": lax.rem(iz + k, nz)}, device_id_type=pl.DeviceIdType.MESH)
    for k in range(1, chips):
        pl.semaphore_signal(
            barrier, 1, device_id={"dout": 2 * lax.rem(chip + k, chips) + core}, device_id_type=pl.DeviceIdType.MESH
        )
    pl.semaphore_signal(barrier, 1, device_id={"dout": mate}, device_id_type=pl.DeviceIdType.MESH)
    chip_by = chip + 1 - 2 * (chip % 2)
    pl.semaphore_signal(barrier, 1, device_id={"dout": 2 * chip_by + 1 - core}, device_id_type=pl.DeviceIdType.MESH)

    for c in range(nc):
        pltpu.make_async_copy(
            gy_hbm.at[:, pl.ds(c * LANES, LANES)], gyf.at[c, rows_of(iz)], loc_sem.at[c]
        ).wait()
    pltpu.make_async_copy(x_hbm, xf.at[jd], loc_sem.at[nc]).wait()
    pl.semaphore_wait(barrier, nz - 1 + chips - 1 + 2)

    def send_right(s, c):
        block = lax.rem(iz - s + nz, nz)
        part = gyf.at[c, rows_of(block)]
        return remote(part, part, gy_send.at[0, s], gy_recv.at[0, s, c], din=right)

    def send_left(s, c):
        block = lax.rem(iz + s, nz)
        part = gyf.at[c, rows_of(block)]
        return remote(part, part, gy_send.at[1, s], gy_recv.at[1, s, c], din=left)

    for c in range(nc):
        if half > 1 or c < cl:
            send_right(0, c).start()
        if half > 1 or c >= cl:
            send_left(0, c).start()

    def x_copy(k, dev, sem):
        return remote(xf.at[k], xf.at[k], x_send.at[sem], x_recv.at[k], dout=dev)

    x_copy(jd, mate, 2 * chips - 2).start()
    for k in range(1, chips):
        x_copy(jd, 2 * lax.rem(chip + k, chips) + core, k - 1).start()

    def x_forward(k):
        src = 2 * lax.rem(chip + chips - k, chips) + core
        x_copy(src, mate, chips - 1 + k - 1).wait_recv()
        x_copy(src, mate, chips - 1 + k - 1).start()

    def ring(r, c, last=False):
        bl = lax.rem(iz - r + nz, nz)
        br = lax.rem(iz + r, nz)
        if not last or c < cl:
            part = gyf.at[c, rows_of(bl)]
            remote(part, part, gy_send.at[0, 0], gy_recv.at[0, r - 1, c], din=right).wait_recv()
            if not last:
                if c < cl:
                    send_right(r, c).start()
                else:
                    @pl.when(r < half - 1)
                    def _():
                        send_right(r, c).start()
        if not last or c >= cl:
            part = gyf.at[c, rows_of(br)]
            remote(part, part, gy_send.at[1, 0], gy_recv.at[1, r - 1, c], din=left).wait_recv()
            if not last:
                if c >= cl:
                    send_left(r, c).start()
                else:
                    @pl.when(r < half - 1)
                    def _():
                        send_left(r, c).start()

    def lookup(which, idx):
        low = lax.bitwise_and(idx, LANES - 1)
        first = jnp.take_along_axis(table[which, :, 0:LANES], low, axis=1, mode="promise_in_bounds")
        second = jnp.take_along_axis(table[which, :, LANES:KCODE], low, axis=1, mode="promise_in_bounds")
        return jnp.where(idx >= LANES, second, first)

    def decode(c):
        cols = pl.ds(c * LANES, LANES)
        co = coef[0:1, cols]

        @pl.loop(0, groups // 8)
        def _(q):
            at = pl.ds(pl.multiple_of(q * 8, 8), 8)
            c0 = codes[0, at, cols]
            c1 = codes[1, at, cols]
            out = []
            for g in range(8):
                d = lookup(0, jnp.broadcast_to(c0[g : g + 1], (8, LANES))) + lookup(
                    1, jnp.broadcast_to(c1[g : g + 1], (8, LANES))
                )
                out.append(d)
            d = jnp.concatenate(out, axis=0)
            where = pl.ds(pl.multiple_of(q * 64, 64), 64)
            dec[where, cols] = d
            wts[where, cols] = (d * co).astype(bf16)

    def g_part(block, slot):
        lhs = jnp.concatenate([gyf[c, rows_of(block)] for c in range(nc)], axis=1)
        g = lax.dot_general(lhs, wts[...], (((1,), (1,)), ((), ())), preferred_element_type=f32)
        g = g.reshape(2, rows // 2, feats)
        gkeep[slot] = g
        gst[slot] = g.astype(bf16)
        remote(gst.at[slot, 1 - core], gpr.at[slot], p_send.at[slot], p_recv.at[slot], dout=mate).start()

    def g_pass(block, slot):
        remote(gst.at[slot, 1 - core], gpr.at[slot], p_send.at[slot], p_recv.at[slot], dout=mate).wait_recv()
        total = gkeep[slot, core] + gpr[slot].astype(f32)
        rss[slot] = total.astype(bf16)

        @pl.when(block == chip)
        def _():
            pltpu.make_async_copy(rss.at[slot], rsr.at[chip], r_send.at[slot]).start()

        @pl.when(block != chip)
        def _():
            remote(rss.at[slot], rsr.at[chip], r_send.at[slot], r_recv.at[chip], dout=2 * block + core).start()

    def left_of(r):
        return lax.rem(iz - r + nz, nz)

    def right_of(r):
        return lax.rem(iz + r, nz)

    def gw_pair(q, first=False):
        b0, b1 = right_of(q), left_of(q + 1)
        lhs = jnp.concatenate([xt[b0], xt[b1]], axis=1)
        for c in range(nc):
            gw_chunk(lhs, b0, b1, c, first)

    def gw_chunk(lhs, b0, b1, c, first=False):
        rhs = jnp.concatenate([gyf[c, rows_of(b0)], gyf[c, rows_of(b1)]], axis=0)
        d = jnp.dot(lhs, rhs, preferred_element_type=f32)
        cols = pl.ds(c * LANES, LANES)
        if first:
            gw[:, cols] = d
        else:
            gw[:, cols] += d

    def transpose_x(k):
        blk = xf[pl.ds(2 * k, 2)].reshape(rows, feats)
        xt[k] = jnp.transpose(blk)

    if half > 1:
        for c in range(nc):
            ring(1, c)
            decode(c)
    else:
        for c in range(nc):
            decode(c)
    g_part(iz, 0)

    fw = list(range(1, chips))
    if half > 2:
        for c in range(nc):
            ring(2, c)
            for k in fw[c::nc]:
                x_forward(k)
            if c == nc // 2 - 1:
                g_part(left_of(1), 1)
            if c == nc - 1:
                g_part(right_of(1), 2)
    else:
        for k in fw:
            x_forward(k)
        if half > 1:
            g_part(left_of(1), 1)
            g_part(right_of(1), 2)
    g_pass(iz, 0)

    def x_ready(k):
        src = 2 * k + 1 - core
        x_copy(src, mate, 0).wait_recv()
        transpose_x(k)

    if half > 3:
        for c in range(nc):
            ring(3, c)
            for k in range(c, chips, nc):
                x_ready(k)
            if c == 2 % nc:
                g_part(left_of(2), 3)
            if c == 4 % nc:
                g_part(right_of(2), 4)
        g_pass(left_of(1), 1)
        g_pass(right_of(1), 2)
    else:
        for k in range(chips):
            x_ready(k)
        for r in range(2, half):
            g_part(left_of(r), 2 * r - 1)
            g_part(right_of(r), 2 * r)
        for r in range(1, min(half, 2)):
            g_pass(left_of(r), 2 * r - 1)
            g_pass(right_of(r), 2 * r)

    gw_pair(0, True)
    if half > 4:
        @pl.loop(4, half)
        def _(r):
            for c in range(nc):
                ring(r, c)
                if c == 1:
                    g_part(left_of(r - 1), 2 * r - 3)
                if c == 2:
                    g_part(right_of(r - 1), 2 * r - 2)
                if c == 3:
                    gw_pair(r - 2)
                if c == 4:
                    @pl.when(r == 4)
                    def _():
                        gw_pair(1)
                if c == 5:
                    g_pass(left_of(r - 2), 2 * r - 5)
                    g_pass(right_of(r - 2), 2 * r - 4)

        done = half - 2
    else:
        done = 1

    if half > 3:
        g_part(left_of(half - 1), 2 * half - 3)
        g_part(right_of(half - 1), 2 * half - 2)
        g_pass(left_of(half - 2), 2 * half - 5)
        g_pass(right_of(half - 2), 2 * half - 4)
    for q in range(done, half - 1):
        gw_pair(q)
    if half > 2:
        g_pass(left_of(half - 1), 2 * half - 3)
        g_pass(right_of(half - 1), 2 * half - 2)

    hloc[...] = jnp.zeros_like(hloc)
    sown[...] = jnp.zeros_like(sown)
    order = []
    for k in range(cl):
        order.append(k)
        if cl + k < nc:
            order.append(cl + k)
    b0, b1 = right_of(half - 1), left_of(half)
    lhs = jnp.concatenate([xt[b0], xt[b1]], axis=1)
    row_low = lax.broadcasted_iota(jnp.int32, (LOW * 8, LANES), 0) // 8
    row_high = lax.broadcasted_iota(jnp.int32, (HIGH, LANES), 0)

    def finish(c):
        cols = pl.ds(c * LANES, LANES)
        sown[c : c + 1, :] = jnp.sum(dec[:, cols] * gw[:, cols], axis=0, keepdims=True)
        co = coef[0:1, cols]

        @pl.loop(0, groups // 8)
        def _(q):
            at = pl.ds(pl.multiple_of(q * 8, 8), 8)
            s = gw[pl.ds(pl.multiple_of(q * 64, 64), 64), cols] * co
            for b in range(BOOKS):
                cd = codes[b, at, cols]
                lo = lax.bitwise_and(cd, LOW - 1)
                hi = lax.shift_right_logical(cd, 3)
                a, o = [], []
                for g in range(8):
                    sg = s[8 * g : 8 * g + 8]
                    rep = jnp.concatenate([sg] * LOW, axis=0)
                    lo_b = jnp.broadcast_to(lo[g : g + 1], (LOW * 8, LANES))
                    a.append(jnp.where(lo_b == row_low, rep, 0.0).astype(bf16))
                    hi_b = jnp.broadcast_to(hi[g : g + 1], (HIGH, LANES))
                    o.append(jnp.where(hi_b == row_high, 1.0, 0.0).astype(bf16))
                left_m = jnp.concatenate(a, axis=1)
                right_m = jnp.concatenate(o, axis=1)
                hloc[b] += lax.dot_general(
                    left_m, right_m, (((1,), (1,)), ((), ())), preferred_element_type=f32
                )

    for c in order:
        ring(half, c, last=True)
        gw_chunk(lhs, b0, b1, c)
        if c == order[-1]:
            g_part(left_of(half), 2 * half - 1)
        finish(c)

    def s_copy(k):
        dev = lax.rem(iz + k, nz)
        return remote(sown, sz.at[iz], s_send.at[k - 1], s_recv.at[iz], din=dev)

    for k in range(1, nz):
        s_copy(k).start()

    pair = remote(hloc.at[1 - core], hpair, hp_send, hp_recv, dout=mate)
    pair.start()
    g_pass(left_of(half), 2 * half - 1)
    pair.wait_recv()
    both = hloc[core] + hpair[...]
    hsum[0] = both[0 : LOW * 4]
    hsum[1] = both[LOW * 4 : LOW * 8]

    def h_copy(k):
        other = lax.rem(chip + k, chips)
        return remote(
            hsum.at[other % 2], hplane.at[chip], hx_send.at[k - 1], hx_recv.at[chip], dout=2 * other + core
        )

    for k in range(1, chips):
        h_copy(k).start()
    hplane[chip] = hsum[chip % 2]
    for k in range(1, chips):
        src = lax.rem(chip + chips - k, chips)
        remote(hsum.at[0], hplane.at[src], hx_send.at[0], hx_recv.at[src], dout=2 * src + core).wait_recv()
    hz[iz] = jnp.sum(hplane[...], axis=0)

    def z_copy(k):
        dev = lax.rem(iz + k, nz)
        return remote(hz.at[iz], hz.at[iz], hz_send.at[k - 1], hz_recv.at[iz], din=dev)

    for k in range(1, nz):
        z_copy(k).start()

    sz[iz] = sown[...]
    for k in range(1, nz):
        src = lax.rem(iz + nz - k, nz)
        remote(sown, sz.at[src], s_send.at[0], s_recv.at[src], din=src).wait_recv()
    scale_out[...] = jnp.sum(sz[...], axis=0)

    for k in range(1, chips):
        src = lax.rem(chip + chips - k, chips)
        remote(rss.at[0], rsr.at[src], r_send.at[0], r_recv.at[src], dout=2 * src + core).wait_recv()
    slot_own = 0
    dist = lax.rem(chip - iz + nz, nz)
    slot_own = jnp.where(dist == 0, 0, jnp.where(dist < half, 2 * dist, 2 * (nz - dist) - 1))
    pltpu.make_async_copy(rss.at[slot_own], rsr.at[chip], r_send.at[slot_own]).wait()
    acc = rsr[0].astype(f32)
    for k in range(1, chips):
        acc = acc + rsr[k].astype(f32)
    gx_out[...] = acc

    for k in range(1, nz):
        src = lax.rem(iz + nz - k, nz)
        remote(hz.at[src], hz.at[src], hz_send.at[0], hz_recv.at[src], din=src).wait_recv()
    mine = 2 * core + chip % 2
    hfin[mine] = jnp.sum(hz[...], axis=0)

    def f_copy(k):
        if k == 0:
            dev = mate
        elif k == 1:
            dev = 2 * chip_by + core
        else:
            dev = 2 * chip_by + 1 - core
        return remote(hfin.at[mine], hfin.at[mine], hf_send.at[k], hf_recv.at[mine], dout=dev)

    for k in range(3):
        f_copy(k).start()
    for k in range(1, 4):
        src = lax.rem(mine + k, 4)
        remote(hfin.at[src], hfin.at[src], hf_send.at[0], hf_recv.at[src], dout=mate).wait_recv()
    book_out[...] = hfin[...]

    for s in range(half):
        wr = gyf.at[pl.ds(0, nc if s < half - 1 else cl), rows_of(left_of(s))]
        remote(wr, wr, gy_send.at[0, s], gy_recv.at[0, s, 0], din=right).wait_send()
        if s < half - 1:
            wl = gyf.at[:, rows_of(right_of(s))]
        else:
            wl = gyf.at[pl.ds(cl, nc - cl), rows_of(right_of(s))]
        if s < half - 1 or nc > cl:
            remote(wl, wl, gy_send.at[1, s], gy_recv.at[1, s, 0], din=left).wait_send()
    for k in range(2 * chips - 1):
        x_copy(jd, mate, k).wait_send()
    for k in range(1, nz):
        s_copy(k).wait_send()
        z_copy(k).wait_send()
    for k in range(1, chips):
        h_copy(k).wait_send()
    pair.wait_send()
    for k in range(3):
        f_copy(k).wait_send()
    for k in range(nz):
        remote(gst.at[k, 1 - core], gpr.at[k], p_send.at[k], p_recv.at[k], dout=mate).wait_send()

        @pl.when(k != slot_own)
        def _():
            remote(rss.at[k], rsr.at[chip], r_send.at[k], r_recv.at[chip], dout=mate).wait_send()


def fused(nz, nd, x, gy, codes, table, coef):
    xrows, feats = x.shape
    rows, outs = gy.shape
    nc = outs // LANES
    chips = nd // 2
    half = nz // 2
    bf16, f32 = jnp.bfloat16, jnp.float32
    V = pltpu.VMEM
    D = pltpu.SemaphoreType.DMA
    vm = pl.BlockSpec(memory_space=pltpu.VMEM)
    anyspec = pl.BlockSpec(memory_space=pl.ANY)
    tile = (LOW * 4, HIGH)
    scratch = [
        V((nc, rows * nz, LANES), bf16),
        V((nd, xrows, feats), bf16),
        V((nz, feats, rows), bf16),
        V((feats, outs), bf16),
        V((feats, outs), f32),
        V((feats, outs), f32),
        V((nz, 2, rows // 2, feats), f32),
        V((nz, 2, rows // 2, feats), bf16),
        V((nz, rows // 2, feats), bf16),
        V((nz, rows // 2, feats), bf16),
        V((chips, rows // 2, feats), bf16),
        V((BOOKS, LOW * 8, HIGH), f32),
        V((LOW * 8, HIGH), f32),
        V((2,) + tile, f32),
        V((chips,) + tile, f32),
        V((nz,) + tile, f32),
        V((4,) + tile, f32),
        V((8, LANES), f32),
        V((nz, 8, LANES), f32),
        D((nc + 1,)),
        D((2, half)),
        D((2, half, nc)),
        D((2 * chips - 1,)),
        D((nd,)),
        D((nz,)),
        D((nz,)),
        D((nz,)),
        D((chips,)),
        D(()),
        D(()),
        D((chips,)),
        D((chips,)),
        D((nz,)),
        D((nz,)),
        D((3,)),
        D((4,)),
        D((nz,)),
        D((nz,)),
    ]
    return pl.pallas_call(
        functools.partial(kernel, nz, nd),
        out_shape=(
            jax.ShapeDtypeStruct((xrows, feats), f32),
            jax.ShapeDtypeStruct((4,) + tile, f32),
            jax.ShapeDtypeStruct((8, LANES), f32),
        ),
        in_specs=[anyspec, anyspec, vm, vm, vm],
        out_specs=(vm, vm, vm),
        scratch_shapes=scratch,
        compiler_params=pltpu.CompilerParams(
            collective_id=0, has_side_effects=True, vmem_limit_bytes=60 * 1024 * 1024
        ),
        name="fused",
    )(x, gy, codes, table, coef)


def local(nz, nd, inputs, cotangent, codes, codebooks, scales, book_mean, book_var, scale_mean, scale_var):
    norm_factor = 1.0 / (2.0 * DOUT) ** 0.5
    loss_scale = (TOKENS * DIN / 4096.0) ** 0.5
    coef = scales * norm_factor
    outs = scales.shape[0]
    table = jnp.transpose(codebooks, (0, 2, 1)).astype(jnp.bfloat16).astype(jnp.float32)
    gx, book, scale = fused(nz, nd, inputs, cotangent, codes, table, coef.reshape(1, outs))
    book = book.reshape(BOOKS, LOW, GROUP, HIGH)
    grad_sums = jnp.transpose(book, (0, 3, 1, 2)).reshape(BOOKS, KCODE, GROUP)
    book_grad = grad_sums / loss_scale
    scale_grad = scale[: outs // LANES].reshape(outs) * norm_factor / loss_scale
    new_books, new_book_mean, new_book_var = adam_step(codebooks, book_mean, book_var, book_grad)
    new_scales, new_scale_mean, new_scale_var = adam_step(scales, scale_mean, scale_var, scale_grad)
    return (
        gx.astype(jnp.bfloat16),
        book_grad,
        new_books,
        new_book_mean,
        new_book_var,
        new_scales,
        new_scale_mean,
        new_scale_var,
    )


def solution(mesh):
    nz, nd = mesh.shape["din"], mesh.shape["dout"]
    in_specs = (
        P("dout", "din"),
        P("din", "dout"),
        P(None, "din", "dout"),
        P(),
        P("dout"),
        P(),
        P(),
        P("dout"),
        P("dout"),
    )
    out_specs = (P("dout", "din"), P(), P(), P(), P(), P("dout"), P("dout"), P("dout"))
    return jax.shard_map(
        functools.partial(local, nz, nd), mesh=mesh, in_specs=in_specs, out_specs=out_specs, check_vma=False
    )
```

time: 396 us -> 116 us (0.29)
  blocking collectives: 139 us -> 0 us
  waiting for transfers between devices: 136 us -> 0 us
  Pallas kernels: 0 us -> 108 us
  matrix products: 80.8 us -> 0 us
  local copies, waits for them, and re-layouts: 19.7 us -> 2.73 us
  between operations: 13.8 us -> 0.73 us
    psum x2 -> x0, blocking collectives: 139 us -> none  [the longest x1 117 us: local(): grad_sums = lax.psum(grad_total, ('din', 'dout'))]
    all_gather x2 -> x0, waiting for transfers between devices: 134 us -> none  [the longest x1 68.8 us: local(): gy_full = lax.all_gather(cotangent, 'din', axis=0, tiled=True)]
    pallas_call x0 -> x1, Pallas kernels: none -> 108 us  [fused(): pl.pallas_call(functools.partial(kernel, nz, nd), out_shape=(jax.ShapeDty...]
    dot_general x66 -> x0, matrix products: 80.8 us -> none  [the longest x32 47.3 us: decode_block(): jnp.einsum('kgo,gjo->kj', onehot, scaled_block, preferred_element_type=jn...]
    eq x16 -> x0, local copies, waits for them, and re-layouts: 12.5 us -> none  [decode_block(): onehot = (code_block[which_book][None] == code_iota).astype(jnp.bfloat16)]
    unnamed x15 -> x18, local copies, waits for them, and re-layouts: 7.16 us -> 1.27 us
  transfers between devices with their start and end apart: 3 -> 0, of which waited for: 2 -> 0; matrix products, arithmetic and copies ran while one was open for 1% -> 0% of each run, Pallas kernels for 0% -> 0%
where the time goes in v1:
time: 116 us; the launch traced here: 115 us
  Pallas kernels  108 us (93%)
  other arithmetic  4.17 us (4%)
  local copies, waits for them, and re-layouts  2.73 us (2%)
    pallas_call x1, Pallas kernels, fused(): pl.pallas_call(functools.partial(kernel, nz, nd), out_shape=(jax.ShapeDty...  108 us

profile of v1, /device:TPU:1, one launch (start us, length us, event | category | flops | bytes accessed | tf_op | source)
XLA Modules:
  0.0 115.5 jit_solution(3086689624693074677)
XLA Ops:
  0.6 0.0 copy-start.5
  0.6 1.3 %convert_bitcast_fusion.table = f32[2,8,256]{2,1,0:T(8,128)} fusion(f32[2,256,8]{1,2,0:T(8,128)} %param.12), kind=kLoop, calls=%fused_computation.3 | loop fusion | flops 8192 | bytes 32768 | tf_op jit(solution)/shard_map/convert_element_type | solution.py:533
  2.0 0.0 copy-done.5
  2.0 0.6 reshape.41.coef
  2.6 107.8 %fused.1 = (f32[64,512]{1,0:T(8,128)}, f32[4,32,32]{2,1,0:T(8,128)}, f32[8,128]{1,0:T(8,128)}) custom-call(bf16[64,512]{1,0:T(8,128)(2,1)} %x_hbm.1, bf16[128,896]{1,0:T(8,128)(2,1)} %gy_hbm.1, s32[2,64,896]{2,1,0:T(8,128)} %codes.1, f32[2,8,256]{2,1,0:T(8,128)} %convert_bitcast_fusion.table, f32[1,896]{1,0:T(1,128)} %reshape.41.coef), custom_call_target="tpu_custom_call" | custom-call | tf_op jit(solution)/shard_map/fused/pallas_call | solution.py:511
  110.4 0.0 copy-start.2
  110.4 1.6 %convert_element_type.15 = bf16[64,512]{1,0:T(8,128)(2,1)} convert(f32[64,512]{1,0:T(8,128)} %get-tuple-element.11) | non-fusion elementwise | flops 32768 | bytes 196608 | tf_op jit(solution)/shard_map/convert_element_type | solution.py:542
  112.0 0.1 copy.20
  112.2 0.2 div.52
  112.3 0.0 copy-start
  112.3 0.1 copy.21
  112.5 0.2 mul.102
  112.6 0.1 copy.22
  112.8 0.0 copy-start.1
  112.8 0.0 copy-start.3
  112.8 0.0 copy-start.4
  112.8 0.2 mul.109
  113.0 0.5 copy-done.1
  113.5 0.0 copy-done.3
  113.5 0.0 copy-done.4
  113.5 0.6 multiply_subtract_fusion
  114.2 0.1 copy-done.7
  114.2 0.6 copy-done.6
  114.8 0.6 multiply_subtract_fusion.1
  (8 shorter events, 0.0 us)
Async XLA Ops:
  0.6 1.3 %copy-start.5 = (f32[896]{0:T(1024)S(1)}, f32[896]{0:T(1024)}, u32[]{:S(2)}) copy-start(f32[896]{0:T(1024)} %param.13) | copy-start | bytes 10756
  110.4 1.6 %copy-start.2 = (f32[4,32,32]{2,1,0:T(8,128)S(1)}, f32[4,32,32]{2,1,0:T(8,128)}, u32[]{:S(2)}) copy-start(f32[4,32,32]{2,1,0:T(8,128)} %get-tuple-element.12) | copy-start | bytes 49156
  112.3 0.7 copy-start
  112.8 0.7 copy-start.1
  112.8 0.7 copy-start.3
  112.8 0.7 copy-start.4
  113.5 0.7 copy-start.7
  113.5 0.7 copy-start.8
  114.2 0.7 copy-start.6

commit v2 on v1

v2 whole, which is shorter than its diff:
```python
import functools

import jax
import jax.numpy as jnp
from jax import lax
from jax.experimental import pallas as pl
from jax.experimental.pallas import tpu as pltpu
from jax.sharding import PartitionSpec as P

DIN = 8192
DOUT = 28672
KCODE = 256
BOOKS = 2
GROUP = 8
TOKENS = 2048

beta_one = 0.9
beta_two = 0.999
adam_rate = 0.01
adam_eps = 1e-08
corr_one = 1.0 - 0.9**10
corr_two = 1.0 - 0.999**10

LANES = 128
LOW = 8
HBITS = 5
SKEW = 1
UNROLL = 16
HIGH = KCODE // LOW


def adam_step(param, mean_old, var_old, gradient):
    mean_new = beta_one * mean_old + (1.0 - beta_one) * gradient
    var_new = beta_two * var_old + (1.0 - beta_two) * gradient * gradient
    update = mean_new / corr_one / (jnp.sqrt(var_new / corr_two) + adam_eps)
    return (param - adam_rate * update, mean_new, var_new)


def kernel(
    nz, nd, x_hbm, gy_hbm, codes_hbm, books_hbm, scales_hbm, gx_out, book_out, scale_out,
    codes, books, scales, gyf, xf, xt, wts, dec, gw, table, gkeep, gst, gpr, rss, rsr, hloc, hbk, hplane, hz, hfin, sown, sz,
    loc_sem, gy_send, gy_recv, x_send, x_recv, p_send, p_recv, r_send, r_recv,
    hx_send, hx_recv, hz_send, hz_recv, hf_send, hf_recv, s_send, s_recv,
):
    chips = nd // 2
    half = nz // 2
    nc = gyf.shape[0]
    early = list(range((nc + 1) // 2))
    late = list(range((nc + 1) // 2, nc))
    goes_right = [k % 2 == 0 for k in range(nc)]
    n_right = sum(goes_right)
    skew = min(SKEW, half - 1)
    rows = gy_hbm.shape[0]
    xrows = x_hbm.shape[0]
    feats = x_hbm.shape[1]
    groups = codes.shape[1]
    iz = lax.axis_index("din")
    jd = lax.axis_index("dout")
    chip = jd // 2
    core = jd % 2
    mate = jd + 1 - 2 * core
    right = lax.rem(iz + 1, nz)
    left = lax.rem(iz + nz - 1, nz)
    f32 = jnp.float32
    bf16 = jnp.bfloat16

    def remote(src, dst, ssem, rsem, din=None, dout=None):
        where = {}
        if din is not None:
            where["din"] = din
        if dout is not None:
            where["dout"] = dout
        return pltpu.make_async_remote_copy(
            src_ref=src, dst_ref=dst, send_sem=ssem, recv_sem=rsem,
            device_id=where, device_id_type=pl.DeviceIdType.MESH,
        )

    def rows_of(block):
        return pl.ds(pl.multiple_of(block * rows, rows), rows)

    for c in range(nc):
        pltpu.make_async_copy(
            gy_hbm.at[:, pl.ds(c * LANES, LANES)], gyf.at[c, rows_of(iz)], loc_sem.at[c]
        ).start()
    pltpu.make_async_copy(x_hbm, xf.at[jd], loc_sem.at[nc]).start()
    operands = ((codes_hbm, codes), (books_hbm, books), (scales_hbm, scales))
    for n, (src, dst) in enumerate(operands):
        pltpu.make_async_copy(src, dst, loc_sem.at[nc + 1 + n]).start()

    barrier = pltpu.get_barrier_semaphore()
    for k in range(1, nz):
        pl.semaphore_signal(barrier, 1, device_id={"din": lax.rem(iz + k, nz)}, device_id_type=pl.DeviceIdType.MESH)
    for k in range(1, nd):
        pl.semaphore_signal(barrier, 1, device_id={"dout": lax.rem(jd + k, nd)}, device_id_type=pl.DeviceIdType.MESH)

    norm_factor = 1.0 / (2.0 * DOUT) ** 0.5
    def coef_of(c):
        return scales[pl.ds(c * LANES, LANES)].reshape(1, LANES) * norm_factor

    def lookup(which, idx):
        low = lax.bitwise_and(idx, LANES - 1)
        first = jnp.take_along_axis(table[which, :, 0:LANES], low, axis=1, mode="promise_in_bounds")
        second = jnp.take_along_axis(table[which, :, LANES:KCODE], low, axis=1, mode="promise_in_bounds")
        return jnp.where(idx >= LANES, second, first)

    unroll = min(UNROLL, groups)

    def decode(c):
        cols = pl.ds(c * LANES, LANES)
        co = coef_of(c)

        @pl.loop(0, groups // unroll)
        def _(q):
            at = pl.ds(pl.multiple_of(q * unroll, unroll), unroll)
            c0 = codes[0, at, cols]
            c1 = codes[1, at, cols]
            out = []
            for g in range(unroll):
                d = lookup(0, jnp.broadcast_to(c0[g : g + 1], (8, LANES))) + lookup(
                    1, jnp.broadcast_to(c1[g : g + 1], (8, LANES))
                )
                out.append(d)
            d = jnp.concatenate(out, axis=0)
            where = pl.ds(pl.multiple_of(q * unroll * 8, unroll * 8), unroll * 8)
            dec[where, cols] = d
            wts[where, cols] = (d * co).astype(bf16)

    for c in range(nc):
        pltpu.make_async_copy(
            gy_hbm.at[:, pl.ds(c * LANES, LANES)], gyf.at[c, rows_of(iz)], loc_sem.at[c]
        ).wait()
    pltpu.make_async_copy(x_hbm, xf.at[jd], loc_sem.at[nc]).wait()
    pl.semaphore_wait(barrier, nz - 1 + nd - 1)

    def send_right(s, c):
        block = lax.rem(iz - s + nz, nz)
        part = gyf.at[c, rows_of(block)]
        return remote(part, part, gy_send.at[0, s], gy_recv.at[0, s, c], din=right)

    def send_left(s, c):
        block = lax.rem(iz + s, nz)
        part = gyf.at[c, rows_of(block)]
        return remote(part, part, gy_send.at[1, s], gy_recv.at[1, s, c], din=left)

    def send_own(c):
        if half > 1 or goes_right[c]:
            send_right(0, c).start()
        if half > 1 or not goes_right[c]:
            send_left(0, c).start()

    for c in range(nc):
        send_own(c)

    def x_copy(k, dev, sem):
        return remote(xf.at[k], xf.at[k], x_send.at[sem], x_recv.at[k], dout=dev)

    x_copy(jd, mate, 2 * chips - 2).start()
    for k in range(1, chips):
        x_copy(jd, 2 * lax.rem(chip + k, chips) + core, k - 1).start()

    def x_forward(k):
        src = 2 * lax.rem(chip + chips - k, chips) + core
        x_copy(src, mate, chips - 1 + k - 1).wait_recv()
        x_copy(src, mate, chips - 1 + k - 1).start()

    def ring(r, c):
        bl = lax.rem(iz - r + nz, nz)
        br = lax.rem(iz + r, nz)
        if r < half or goes_right[c]:
            part = gyf.at[c, rows_of(bl)]
            remote(part, part, gy_send.at[0, 0], gy_recv.at[0, r - 1, c], din=right).wait_recv()
            if r < half - 1 or (r == half - 1 and goes_right[c]):
                send_right(r, c).start()
        if r < half or not goes_right[c]:
            part = gyf.at[c, rows_of(br)]
            remote(part, part, gy_send.at[1, 0], gy_recv.at[1, r - 1, c], din=left).wait_recv()
            if r < half - 1 or (r == half - 1 and not goes_right[c]):
                send_left(r, c).start()

    def g_dot(block, chunks):
        lhs = jnp.concatenate([gyf[c, rows_of(block)] for c in chunks], axis=1)
        rhs = wts[:, pl.ds(chunks[0] * LANES, len(chunks) * LANES)]
        return lax.dot_general(lhs, rhs, (((1,), (1,)), ((), ())), preferred_element_type=f32)

    def g_early(block, slot):
        gkeep[slot] = g_dot(block, early).reshape(2, rows // 2, feats)

    def g_late(block, slot):
        g = gkeep[slot] + g_dot(block, late).reshape(2, rows // 2, feats)
        gkeep[slot] = g
        gst[slot] = g.astype(bf16)
        remote(gst.at[slot, 1 - core], gpr.at[slot], p_send.at[slot], p_recv.at[slot], dout=mate).start()

    def g_pass(block, slot):
        remote(gst.at[slot, 1 - core], gpr.at[slot], p_send.at[slot], p_recv.at[slot], dout=mate).wait_recv()
        total = gkeep[slot, core] + gpr[slot].astype(f32)
        rss[slot] = total.astype(bf16)

        @pl.when(block == chip)
        def _():
            pltpu.make_async_copy(rss.at[slot], rsr.at[chip], r_send.at[slot]).start()

        @pl.when(block != chip)
        def _():
            remote(rss.at[slot], rsr.at[chip], r_send.at[slot], r_recv.at[chip], dout=2 * block + core).start()

    def left_of(r):
        return lax.rem(iz - r + nz, nz)

    def right_of(r):
        return lax.rem(iz + r, nz)

    def gw_pair(q, chunks):
        b0, b1 = right_of(q), left_of(q + 1)
        lhs = jnp.concatenate([xt[b0], xt[b1]], axis=1)
        for c in chunks:
            rhs = jnp.concatenate([gyf[c, rows_of(b0)], gyf[c, rows_of(b1)]], axis=0)
            d = jnp.dot(lhs, rhs, preferred_element_type=f32)
            cols = pl.ds(c * LANES, LANES)
            if q == 0:
                gw[:, cols] = d
            else:
                gw[:, cols] += d

    def transpose_x(k):
        blk = xf[pl.ds(2 * k, 2)].reshape(rows, feats)
        xt[k] = jnp.transpose(blk)

    def x_ready(k):
        src = 2 * k + 1 - core
        x_copy(src, mate, 0).wait_recv()
        transpose_x(k)

    hloc[...] = jnp.zeros_like(hloc)
    sown[...] = jnp.zeros_like(sown)
    rows16 = lax.broadcasted_iota(jnp.int32, (16, LANES), 0)
    row_low = [(rows16 // 8 + 2 * n).astype(f32).astype(bf16) for n in range(LOW // 2)]
    row_high = [(rows16 + 16 * n).astype(f32).astype(bf16) for n in range(HIGH // 16)]
    zero16 = jnp.zeros((16, LANES), bf16)
    one16 = jnp.ones((16, LANES), bf16)

    def finish(c):
        cols = pl.ds(c * LANES, LANES)
        sown[c : c + 1, :] = jnp.sum(dec[:, cols] * gw[:, cols], axis=0, keepdims=True)
        co = coef_of(c)

        @pl.loop(0, groups // unroll)
        def _(q):
            at = pl.ds(pl.multiple_of(q * unroll, unroll), unroll)
            s = gw[pl.ds(pl.multiple_of(q * unroll * 8, unroll * 8), unroll * 8), cols] * co
            for b in range(BOOKS):
                cd = codes[b, at, cols]
                lo = lax.shift_right_logical(cd, HBITS).astype(f32)
                hi = lax.bitwise_and(cd, HIGH - 1).astype(f32)
                a, o = [], []
                for g in range(unroll):
                    sg = s[8 * g : 8 * g + 8]
                    two = jnp.concatenate([sg, sg], axis=0).astype(bf16)
                    lo_b = jnp.broadcast_to(lo[g : g + 1], (16, LANES)).astype(bf16)
                    a.append(jnp.concatenate([jnp.where(lo_b == r, two, zero16) for r in row_low], axis=0))
                    hi_b = jnp.broadcast_to(hi[g : g + 1], (16, LANES)).astype(bf16)
                    o.append(jnp.concatenate([jnp.where(hi_b == r, one16, zero16) for r in row_high], axis=0))
                left_m = jnp.concatenate(a, axis=1)
                right_m = jnp.concatenate(o, axis=1)
                hloc[b] += lax.dot_general(
                    right_m, left_m, (((1,), (1,)), ((), ())), preferred_element_type=f32
                )

    for n, (src, dst) in enumerate(operands):
        pltpu.make_async_copy(src, dst, loc_sem.at[nc + 1 + n]).wait()
    for b in range(BOOKS):
        table[b] = books[b].astype(bf16).astype(f32)
    todo = []

    def add(at, job, *args):
        todo.append((at, functools.partial(job, *args)))

    def sides(r):
        pairs = []
        if r == 0:
            pairs.append((lambda: iz, 0))
        else:
            pairs.append((lambda: left_of(r), 2 * r - 1))
            if r < half:
                pairs.append((lambda: right_of(r), 2 * r))
        return pairs

    def on_sides(job, r):
        for block, slot in sides(r):
            job(block(), slot)

    def one_side(job, r, n):
        block, slot = sides(r)[n]
        job(block(), slot)

    for c in range(nc):
        add((0, 0, 1, 1, 1, 2, 2)[c], decode, c)
    for k in range(1, chips):
        add(3, x_forward, k)
    for k in range(chips):
        add(4, x_ready, k)
    when_early = (2, 3, 3, 4, 5, 6, 7, 8, 9)
    when_late = (3, 3, 4, 5, 6, 7, 8, 9, 10)
    for r in range(half + 1):
        for n in range(len(sides(r))):
            add(when_early[r], one_side, g_early, r, n)
    for r in range(half):
        add(when_late[r] + 1, on_sides, g_pass, r)
    for r in range(half + 1):
        for n in range(len(sides(r))):
            add(when_late[r], one_side, g_late, r, n)
    for q in range(half):
        add((5, 5, 5, 6, 6, 7, 8, 9)[q], gw_pair, q, early)
    for q in range(half):
        add((5, 5, 6, 6, 7, 8, 9, 10)[q], gw_pair, q, late)
    for at, job in todo:
        if at == 0:
            job()
    last = half + skew
    for v in range(1, last + 1):
        ops = []
        if v <= half:
            ops += [functools.partial(ring, v, c) for c in early]
        if 1 <= v - skew <= half:
            ops += [functools.partial(ring, v - skew, c) for c in late]
        jobs = [job for at, job in todo if at == v]
        slots = len(ops)
        for n, op in enumerate(ops):
            op()
            for job in jobs[n * len(jobs) // slots : (n + 1) * len(jobs) // slots]:
                job()
    for at, job in todo:
        if at == last + 1:
            job()
    for n, c in enumerate(early + late):
        finish(c)
        if n == 0:
            g_pass(left_of(half), 2 * half - 1)

    def s_copy(k):
        dev = lax.rem(iz + k, nz)
        return remote(sown, sz.at[iz], s_send.at[k - 1], s_recv.at[iz], din=dev)

    for k in range(1, nz):
        s_copy(k).start()

    pieces = hfin.shape[0]
    mine = lax.rem(jd, pieces)
    for b in range(BOOKS):
        turned = jnp.transpose(hloc[b])
        for h in range(2):
            part = jnp.concatenate(
                [turned[8 * n : 8 * n + 8, :] for n in range(LOW // 2 * h, LOW // 2 * (h + 1))], axis=1
            )
            hbk[4 * b + 2 * h] = part[0:4]
            hbk[4 * b + 2 * h + 1] = part[4:8]

    def h_copy(k):
        other = lax.rem(jd + k, nd)
        return remote(
            hbk.at[lax.rem(other, pieces)], hplane.at[jd], hx_send.at[k - 1], hx_recv.at[jd], dout=other
        )

    for k in range(1, nd):
        h_copy(k).start()
    hplane[jd] = hbk[mine]
    for k in range(1, nd):
        src = lax.rem(jd + nd - k, nd)
        remote(hbk.at[0], hplane.at[src], hx_send.at[0], hx_recv.at[src], dout=src).wait_recv()
    hz[iz] = jnp.sum(hplane[...], axis=0)

    def z_copy(k):
        dev = lax.rem(iz + k, nz)
        return remote(hz.at[iz], hz.at[iz], hz_send.at[k - 1], hz_recv.at[iz], din=dev)

    for k in range(1, nz):
        z_copy(k).start()

    sz[iz] = sown[...]
    for k in range(1, nz):
        src = lax.rem(iz + nz - k, nz)
        remote(sown, sz.at[src], s_send.at[0], s_recv.at[src], din=src).wait_recv()
    scale_out[...] = jnp.sum(sz[...], axis=0)

    for k in range(1, chips):
        src = lax.rem(chip + chips - k, chips)
        remote(rss.at[0], rsr.at[src], r_send.at[0], r_recv.at[src], dout=2 * src + core).wait_recv()
    slot_own = 0
    dist = lax.rem(chip - iz + nz, nz)
    slot_own = jnp.where(dist == 0, 0, jnp.where(dist < half, 2 * dist, 2 * (nz - dist) - 1))
    pltpu.make_async_copy(rss.at[slot_own], rsr.at[chip], r_send.at[slot_own]).wait()
    acc = rsr[0].astype(f32)
    for k in range(1, chips):
        acc = acc + rsr[k].astype(f32)
    gx_out[...] = acc.astype(bf16)

    for k in range(1, nz):
        src = lax.rem(iz + nz - k, nz)
        remote(hz.at[src], hz.at[src], hz_send.at[0], hz_recv.at[src], din=src).wait_recv()
    hfin[mine] = jnp.sum(hz[...], axis=0)

    def f_copy(k):
        dev = jd - mine + lax.rem(mine + k, pieces)
        return remote(hfin.at[mine], hfin.at[mine], hf_send.at[k - 1], hf_recv.at[mine], dout=dev)

    for k in range(1, pieces):
        f_copy(k).start()
    for k in range(1, pieces):
        src = lax.rem(mine + k, pieces)
        remote(hfin.at[src], hfin.at[src], hf_send.at[0], hf_recv.at[src], dout=mate).wait_recv()
    for b in range(BOOKS):
        for h in range(2):
            book_out[b, :, pl.ds(h * LANES, LANES)] = jnp.concatenate(
                [hfin[4 * b + 2 * h], hfin[4 * b + 2 * h + 1]], axis=0
            )

    for s in range(half):
        wr = gyf.at[pl.ds(0, nc if s < half - 1 else n_right), rows_of(left_of(s))]
        remote(wr, wr, gy_send.at[0, s], gy_recv.at[0, s, 0], din=right).wait_send()
        if s < half - 1:
            wl = gyf.at[:, rows_of(right_of(s))]
        else:
            wl = gyf.at[pl.ds(0, nc - n_right), rows_of(right_of(s))]
        if s < half - 1 or nc > n_right:
            remote(wl, wl, gy_send.at[1, s], gy_recv.at[1, s, 0], din=left).wait_send()
    for k in range(2 * chips - 1):
        x_copy(jd, mate, k).wait_send()
    for k in range(1, nz):
        s_copy(k).wait_send()
        z_copy(k).wait_send()
    for k in range(1, nd):
        h_copy(k).wait_send()
    for k in range(1, pieces):
        f_copy(k).wait_send()
    for k in range(nz):
        remote(gst.at[k, 1 - core], gpr.at[k], p_send.at[k], p_recv.at[k], dout=mate).wait_send()

        @pl.when(k != slot_own)
        def _():
            remote(rss.at[k], rsr.at[chip], r_send.at[k], r_recv.at[chip], dout=mate).wait_send()


def fused(nz, nd, x, gy, codes, books, scales):
    xrows, feats = x.shape
    rows, outs = gy.shape
    nc = outs // LANES
    chips = nd // 2
    half = nz // 2
    bf16, f32 = jnp.bfloat16, jnp.float32
    V = pltpu.VMEM
    D = pltpu.SemaphoreType.DMA
    vm = pl.BlockSpec(memory_space=pltpu.VMEM)
    anyspec = pl.BlockSpec(memory_space=pl.ANY)
    tile = (GROUP // 2, LANES)
    scratch = [
        V(codes.shape, jnp.int32),
        V(books.shape, f32),
        V(scales.shape, f32),
        V((nc, rows * nz, LANES), bf16),
        V((nd, xrows, feats), bf16),
        V((nz, feats, rows), bf16),
        V((feats, outs), bf16),
        V((feats, outs), f32),
        V((feats, outs), f32),
        V((BOOKS, GROUP, KCODE), f32),
        V((nz, 2, rows // 2, feats), f32),
        V((nz, 2, rows // 2, feats), bf16),
        V((nz, rows // 2, feats), bf16),
        V((nz, rows // 2, feats), bf16),
        V((chips, rows // 2, feats), bf16),
        V((BOOKS, HIGH, LOW * 8), f32),
        V((8,) + tile, f32),
        V((nd,) + tile, f32),
        V((nz,) + tile, f32),
        V((8,) + tile, f32),
        V((8, LANES), f32),
        V((nz, 8, LANES), f32),
        D((nc + 4,)),
        D((2, half)),
        D((2, half, nc)),
        D((2 * chips - 1,)),
        D((nd,)),
        D((nz,)),
        D((nz,)),
        D((nz,)),
        D((chips,)),
        D((nd,)),
        D((nd,)),
        D((nz,)),
        D((nz,)),
        D((8,)),
        D((8,)),
        D((nz,)),
        D((nz,)),
    ]
    return pl.pallas_call(
        functools.partial(kernel, nz, nd),
        out_shape=(
            jax.ShapeDtypeStruct((xrows, feats), bf16),
            jax.ShapeDtypeStruct((BOOKS, GROUP, KCODE), f32),
            jax.ShapeDtypeStruct((8, LANES), f32),
        ),
        in_specs=[anyspec] * 5,
        out_specs=(vm, vm, vm),
        scratch_shapes=scratch,
        compiler_params=pltpu.CompilerParams(
            collective_id=0, has_side_effects=True, vmem_limit_bytes=60 * 1024 * 1024
        ),
        name="fused",
    )(x, gy, codes, books, scales)


def local(nz, nd, inputs, cotangent, codes, codebooks, scales, book_mean, book_var, scale_mean, scale_var):
    norm_factor = 1.0 / (2.0 * DOUT) ** 0.5
    loss_scale = (TOKENS * DIN / 4096.0) ** 0.5
    outs = scales.shape[0]
    gx, book, scale = fused(nz, nd, inputs, cotangent, codes, jnp.transpose(codebooks, (0, 2, 1)), scales)
    book_grad = jnp.transpose(book, (0, 2, 1)) / loss_scale
    scale_grad = scale[: outs // LANES].reshape(outs) * norm_factor / loss_scale
    new_books, new_book_mean, new_book_var = adam_step(codebooks, book_mean, book_var, book_grad)
    new_scales, new_scale_mean, new_scale_var = adam_step(scales, scale_mean, scale_var, scale_grad)
    return (
        gx,
        book_grad,
        new_books,
        new_book_mean,
        new_book_var,
        new_scales,
        new_scale_mean,
        new_scale_var,
    )


def solution(mesh):
    nz, nd = mesh.shape["din"], mesh.shape["dout"]
    in_specs = (
        P("dout", "din"),
        P("din", "dout"),
        P(None, "din", "dout"),
        P(),
        P("dout"),
        P(),
        P(),
        P("dout"),
        P("dout"),
    )
    out_specs = (P("dout", "din"), P(), P(), P(), P(), P("dout"), P("dout"), P("dout"))
    return jax.shard_map(
        functools.partial(local, nz, nd), mesh=mesh, in_specs=in_specs, out_specs=out_specs, check_vma=False
    )
```

time: 116 us -> 95.3 us (0.82)
  Pallas kernels: 108 us -> 91 us
  other arithmetic: 4.17 us -> 2 us
  local copies, waits for them, and re-layouts: 2.73 us -> 1.34 us
    pallas_call x1, Pallas kernels: 108 us -> 91 us  [fused(): pl.pallas_call(functools.partial(kernel, nz, nd), out_shape=(jax.ShapeDty...]
    convert_element_type x2 -> x0, other arithmetic: 2.9 us -> none  [the longest x1 1.57 us: local(): gx.astype(jnp.bfloat16)]
where the time goes in v2:
time: 95.3 us; the launch traced here: 95.1 us
  Pallas kernels  91 us (95%)
  other arithmetic  2 us (2%)
  local copies, waits for them, and re-layouts  1.34 us (1%)
    pallas_call x1, Pallas kernels, fused(): pl.pallas_call(functools.partial(kernel, nz, nd), out_shape=(jax.ShapeDty...  91 us
    sub x2, other arithmetic, adam_step(): return (param - adam_rate * update, mean_new, var_new)  2 us

profile of v2, /device:TPU:1, one launch (start us, length us, event | category | flops | bytes accessed | tf_op | source)
XLA Modules:
  0.0 95.1 jit_solution(3788161039047444004)
XLA Ops:
  0.6 0.0 copy-start.1
  0.6 0.0 copy-start.3
  0.7 0.0 copy-start.4
  0.7 91.0 %fused.1 = (bf16[64,512]{1,0:T(8,128)(2,1)}, f32[2,8,256]{2,1,0:T(8,128)}, f32[8,128]{1,0:T(8,128)}) custom-call(bf16[64,512]{1,0:T(8,128)(2,1)} %x_hbm.1, bf16[128,896]{1,0:T(8,128)(2,1)} %gy_hbm.1, s32[2,64,896]{2,1,0:T(8,128)} %codes_hbm.1, f32[2,8,256]{2,1,0:T(8,128)} %bitcast.18, f32[896]{0:T(1024)} %scales_hbm.1), custom_call_target="tpu_custom_call" | custom-call | tf_op jit(solution)/shard_map/fused/pallas_call | solution.py:496
  91.7 0.0 copy-done.1
  91.7 0.0 copy-done.3
  91.7 0.0 copy-done.4
  91.7 0.0 copy-start.6
  91.7 0.0 copy-start.7
  91.7 0.0 copy-start
  91.8 1.4 %multiply_subtract_fusion = (f32[2,256,8]{1,2,0:T(8,128)}, f32[2,256,8]{1,2,0:T(8,128)}, f32[2,256,8]{1,2,0:T(8,128)}, f32[2,256,8]{1,2,0:T(8,128)}) fusion(f32[2,256,8]{1,2,0:T(8,128)S(1)} %copy-done.1, f32[2,8,256]{2,1,0:T(8,128)} %get-tuple-element.12, f32[2,256,8]{1,2,0:T(8,128)S(1)} %copy-done.3, f32[2,256,8]{1,2,0:T(8,128)S(1)} %copy-done.4), kind=kLoop, calls=%fused_computation.3 | loop fusion | flops 57344 | bytes 131072 | tf_op jit(solution)/shard_map/sub | solution.py:36
  93.1 0.0 copy-start.5
  93.1 0.0 copy-start.2
  93.1 0.0 copy-done.6
  93.2 0.0 copy-done.7
  93.2 0.7 copy-done.5
  93.8 0.0 copy-done.2
  93.8 0.6 multiply_subtract_fusion.1
  94.5 0.0 copy-done
  94.5 0.6 copy.18
Async XLA Ops:
  0.6 91.1 %copy-start.1 = (f32[2,256,8]{1,2,0:T(8,128)S(1)}, f32[2,256,8]{1,2,0:T(8,128)}, u32[]{:S(2)}) copy-start(f32[2,256,8]{1,2,0:T(8,128)} %param.12) | copy-start | bytes 49156
  0.6 91.1 %copy-start.3 = (f32[2,256,8]{1,2,0:T(8,128)S(1)}, f32[2,256,8]{1,2,0:T(8,128)}, u32[]{:S(2)}) copy-start(f32[2,256,8]{1,2,0:T(8,128)} %param.14) | copy-start | bytes 49156
  0.7 91.1 %copy-start.4 = (f32[2,256,8]{1,2,0:T(8,128)S(1)}, f32[2,256,8]{1,2,0:T(8,128)}, u32[]{:S(2)}) copy-start(f32[2,256,8]{1,2,0:T(8,128)} %param.15) | copy-start | bytes 49156
  91.7 1.4 %copy-start.6 = (f32[896]{0:T(1024)S(1)}, f32[896]{0:T(1024)}, u32[]{:S(2)}) copy-start(f32[896]{0:T(1024)} %param.17) | copy-start | bytes 10756
  91.7 1.4 %copy-start.7 = (f32[8,128]{1,0:T(8,128)S(1)}, f32[8,128]{1,0:T(8,128)}, u32[]{:S(2)}) copy-start(f32[8,128]{1,0:T(8,128)} %get-tuple-element.13) | copy-start | bytes 12292
  91.7 2.7 %copy-start = (bf16[64,512]{1,0:T(8,128)(2,1)S(1)}, bf16[64,512]{1,0:T(8,128)(2,1)}, u32[]{:S(2)}) copy-start(bf16[64,512]{1,0:T(8,128)(2,1)} %get-tuple-element.29) | copy-start | bytes 196612
  93.1 0.7 copy-start.5
  93.1 0.7 copy-start.2

commit v3 on v2

--- a/solution.py
+++ b/solution.py
@@ -78,6 +78,12 @@
     def rows_of(block):
         return pl.ds(pl.multiple_of(block * rows, rows), rows)
 
+    barrier = pltpu.get_barrier_semaphore()
+    for dev in (right, left):
+        pl.semaphore_signal(barrier, 1, device_id={"din": dev}, device_id_type=pl.DeviceIdType.MESH)
+    for k in range(1, nd):
+        pl.semaphore_signal(barrier, 1, device_id={"dout": lax.rem(jd + k, nd)}, device_id_type=pl.DeviceIdType.MESH)
+
     for c in range(nc):
         pltpu.make_async_copy(
             gy_hbm.at[:, pl.ds(c * LANES, LANES)], gyf.at[c, rows_of(iz)], loc_sem.at[c]
@@ -86,12 +92,6 @@
     operands = ((codes_hbm, codes), (books_hbm, books), (scales_hbm, scales))
     for n, (src, dst) in enumerate(operands):
         pltpu.make_async_copy(src, dst, loc_sem.at[nc + 1 + n]).start()
-
-    barrier = pltpu.get_barrier_semaphore()
-    for k in range(1, nz):
-        pl.semaphore_signal(barrier, 1, device_id={"din": lax.rem(iz + k, nz)}, device_id_type=pl.DeviceIdType.MESH)
-    for k in range(1, nd):
-        pl.semaphore_signal(barrier, 1, device_id={"dout": lax.rem(jd + k, nd)}, device_id_type=pl.DeviceIdType.MESH)
 
     norm_factor = 1.0 / (2.0 * DOUT) ** 0.5
     def coef_of(c):
@@ -130,7 +130,7 @@
             gy_hbm.at[:, pl.ds(c * LANES, LANES)], gyf.at[c, rows_of(iz)], loc_sem.at[c]
         ).wait()
     pltpu.make_async_copy(x_hbm, xf.at[jd], loc_sem.at[nc]).wait()
-    pl.semaphore_wait(barrier, nz - 1 + nd - 1)
+    pl.semaphore_wait(barrier, 2 + nd - 1)
 
     def send_right(s, c):
         block = lax.rem(iz - s + nz, nz)
@@ -239,13 +239,14 @@
     zero16 = jnp.zeros((16, LANES), bf16)
     one16 = jnp.ones((16, LANES), bf16)
 
-    def finish(c):
+    def scale_part(c):
         cols = pl.ds(c * LANES, LANES)
         sown[c : c + 1, :] = jnp.sum(dec[:, cols] * gw[:, cols], axis=0, keepdims=True)
+
+    def piece(c, q):
+        cols = pl.ds(c * LANES, LANES)
         co = coef_of(c)
-
-        @pl.loop(0, groups // unroll)
-        def _(q):
+        if True:
             at = pl.ds(pl.multiple_of(q * unroll, unroll), unroll)
             s = gw[pl.ds(pl.multiple_of(q * unroll * 8, unroll * 8), unroll * 8), cols] * co
             for b in range(BOOKS):
@@ -266,6 +267,13 @@
                     right_m, left_m, (((1,), (1,)), ((), ())), preferred_element_type=f32
                 )
 
+    def finish(c):
+        scale_part(c)
+
+        @pl.loop(0, groups // unroll)
+        def _(q):
+            piece(c, q)
+
     for n, (src, dst) in enumerate(operands):
         pltpu.make_async_copy(src, dst, loc_sem.at[nc + 1 + n]).wait()
     for b in range(BOOKS):
@@ -304,7 +312,7 @@
     for r in range(half + 1):
         for n in range(len(sides(r))):
             add(when_early[r], one_side, g_early, r, n)
-    for r in range(half):
+    for r in range(half - 1):
         add(when_late[r] + 1, on_sides, g_pass, r)
     for r in range(half + 1):
         for n in range(len(sides(r))):
@@ -335,6 +343,8 @@
     for n, c in enumerate(early + late):
         finish(c)
         if n == 0:
+            on_sides(g_pass, half - 1)
+        if n == 1:
             g_pass(left_of(half), 2 * half - 1)
 
     def s_copy(k):

time: 95.3 us -> 93.3 us (0.979)
  Pallas kernels: 91 us -> 89 us
    pallas_call x1, Pallas kernels: 91 us -> 89 us  [fused(): pl.pallas_call(functools.partial(kernel, nz, nd), out_shape=(jax.ShapeDty...]
where the time goes in v3:
time: 93.3 us; the launch traced here: 93.1 us
  Pallas kernels  89 us (95%)
  other arithmetic  2 us (2%)
  local copies, waits for them, and re-layouts  1.34 us (1%)
    pallas_call x1, Pallas kernels, fused(): pl.pallas_call(functools.partial(kernel, nz, nd), out_shape=(jax.ShapeDty...  89 us
    sub x2, other arithmetic, adam_step(): return (param - adam_rate * update, mean_new, var_new)  2 us

profile of v3, /device:TPU:1, one launch (start us, length us, event | category | flops | bytes accessed | tf_op | source)
XLA Modules:
  0.0 93.1 jit_solution(10498146431442652500)
XLA Ops:
  0.6 0.0 copy-start.1
  0.6 0.0 copy-start.3
  0.7 0.0 copy-start.4
  0.7 89.0 %fused.1 = (bf16[64,512]{1,0:T(8,128)(2,1)}, f32[2,8,256]{2,1,0:T(8,128)}, f32[8,128]{1,0:T(8,128)}) custom-call(bf16[64,512]{1,0:T(8,128)(2,1)} %x_hbm.1, bf16[128,896]{1,0:T(8,128)(2,1)} %gy_hbm.1, s32[2,64,896]{2,1,0:T(8,128)} %codes_hbm.1, f32[2,8,256]{2,1,0:T(8,128)} %bitcast.18, f32[896]{0:T(1024)} %scales_hbm.1), custom_call_target="tpu_custom_call" | custom-call | tf_op jit(solution)/shard_map/fused/pallas_call | solution.py:506
  89.7 0.0 copy-done.1
  89.7 0.0 copy-done.3
  89.7 0.0 copy-done.4
  89.7 0.0 copy-start.6
  89.7 0.0 copy-start.7
  89.7 0.0 copy-start
  89.7 1.4 %multiply_subtract_fusion = (f32[2,256,8]{1,2,0:T(8,128)}, f32[2,256,8]{1,2,0:T(8,128)}, f32[2,256,8]{1,2,0:T(8,128)}, f32[2,256,8]{1,2,0:T(8,128)}) fusion(f32[2,256,8]{1,2,0:T(8,128)S(1)} %copy-done.1, f32[2,8,256]{2,1,0:T(8,128)} %get-tuple-element.12, f32[2,256,8]{1,2,0:T(8,128)S(1)} %copy-done.3, f32[2,256,8]{1,2,0:T(8,128)S(1)} %copy-done.4), kind=kLoop, calls=%fused_computation.3 | loop fusion | flops 57344 | bytes 131072 | tf_op jit(solution)/shard_map/sub | solution.py:36
  91.1 0.0 copy-start.5
  91.1 0.0 copy-start.2
  91.1 0.0 copy-done.6
  91.1 0.0 copy-done.7
  91.2 0.7 copy-done.5
  91.8 0.0 copy-done.2
  91.8 0.6 multiply_subtract_fusion.1
  92.5 0.0 copy-done
  92.5 0.6 copy.18
Async XLA Ops:
  0.6 89.1 %copy-start.1 = (f32[2,256,8]{1,2,0:T(8,128)S(1)}, f32[2,256,8]{1,2,0:T(8,128)}, u32[]{:S(2)}) copy-start(f32[2,256,8]{1,2,0:T(8,128)} %param.12) | copy-start | bytes 49156
  0.6 89.1 %copy-start.3 = (f32[2,256,8]{1,2,0:T(8,128)S(1)}, f32[2,256,8]{1,2,0:T(8,128)}, u32[]{:S(2)}) copy-start(f32[2,256,8]{1,2,0:T(8,128)} %param.14) | copy-start | bytes 49156
  0.7 89.1 %copy-start.4 = (f32[2,256,8]{1,2,0:T(8,128)S(1)}, f32[2,256,8]{1,2,0:T(8,128)}, u32[]{:S(2)}) copy-start(f32[2,256,8]{1,2,0:T(8,128)} %param.15) | copy-start | bytes 49156
  89.7 1.4 %copy-start.6 = (f32[896]{0:T(1024)S(1)}, f32[896]{0:T(1024)}, u32[]{:S(2)}) copy-start(f32[896]{0:T(1024)} %param.17) | copy-start | bytes 10756
  89.7 1.4 %copy-start.7 = (f32[8,128]{1,0:T(8,128)S(1)}, f32[8,128]{1,0:T(8,128)}, u32[]{:S(2)}) copy-start(f32[8,128]{1,0:T(8,128)} %get-tuple-element.13) | copy-start | bytes 12292
  89.7 2.7 %copy-start = (bf16[64,512]{1,0:T(8,128)(2,1)S(1)}, bf16[64,512]{1,0:T(8,128)(2,1)}, u32[]{:S(2)}) copy-start(bf16[64,512]{1,0:T(8,128)(2,1)} %get-tuple-element.29) | copy-start | bytes 196612
  91.1 0.7 copy-start.5
  91.1 0.7 copy-start.2

commit v4 on v3

--- a/solution.py
+++ b/solution.py
@@ -24,7 +24,7 @@
 LANES = 128
 LOW = 8
 HBITS = 5
-SKEW = 1
+SKEW = 2
 UNROLL = 16
 HIGH = KCODE // LOW
 
@@ -38,8 +38,8 @@
 
 def kernel(
     nz, nd, x_hbm, gy_hbm, codes_hbm, books_hbm, scales_hbm, gx_out, book_out, scale_out,
-    codes, books, scales, gyf, xf, xt, wts, dec, gw, table, gkeep, gst, gpr, rss, rsr, hloc, hbk, hplane, hz, hfin, sown, sz,
-    loc_sem, gy_send, gy_recv, x_send, x_recv, p_send, p_recv, r_send, r_recv,
+    codes, books, scales, gyf, xf, xt, wts, dec, gw, table, gkeep, gst, gpr, rss, rsx, rsy, rsr, hloc, hbk, hplane, hz, hfin, sown, sz,
+    loc_sem, gy_send, gy_recv, x_send, x_recv, p_send, p_recv, r_send, r_recv, y_send, y_recv,
     hx_send, hx_recv, hz_send, hz_recv, hf_send, hf_recv, s_send, s_recv,
 ):
     chips = nd // 2
@@ -59,6 +59,8 @@
     chip = jd // 2
     core = jd % 2
     mate = jd + 1 - 2 * core
+    across = rsx.shape[1]
+    my_y, my_x = chip // across, lax.rem(chip, across)
     right = lax.rem(iz + 1, nz)
     left = lax.rem(iz + nz - 1, nz)
     f32 = jnp.float32
@@ -195,14 +197,33 @@
         remote(gst.at[slot, 1 - core], gpr.at[slot], p_send.at[slot], p_recv.at[slot], dout=mate).wait_recv()
         total = gkeep[slot, core] + gpr[slot].astype(f32)
         rss[slot] = total.astype(bf16)
-
-        @pl.when(block == chip)
+        gkeep[slot, core] = total
+        by, bx = block // across, lax.rem(block, across)
+
+        @pl.when(bx != my_x)
         def _():
-            pltpu.make_async_copy(rss.at[slot], rsr.at[chip], r_send.at[slot]).start()
-
-        @pl.when(block != chip)
+            remote(
+                rss.at[slot], rsx.at[by, my_x], r_send.at[slot], r_recv.at[by, my_x],
+                dout=2 * (my_y * across + bx) + core,
+            ).start()
+
+    def g_sum(block, slot):
+        by, bx = block // across, lax.rem(block, across)
+
+        @pl.when(bx == my_x)
         def _():
-            remote(rss.at[slot], rsr.at[chip], r_send.at[slot], r_recv.at[chip], dout=2 * block + core).start()
+            acc = gkeep[slot, core]
+            for k in range(1, across):
+                src = lax.rem(my_x + k, across)
+                remote(
+                    rss.at[slot], rsx.at[by, src], r_send.at[slot], r_recv.at[by, src], dout=mate
+                ).wait_recv()
+                acc = acc + rsx[by, src].astype(f32)
+            rsy[by] = acc.astype(bf16)
+
+            @pl.when(by != my_y)
+            def _():
+                remote(rsy.at[by], rsr.at[my_y], y_send.at[by], y_recv.at[my_y], dout=2 * block + core).start()
 
     def left_of(r):
         return lax.rem(iz - r + nz, nz)
@@ -304,23 +325,31 @@
     for c in range(nc):
         add((0, 0, 1, 1, 1, 2, 2)[c], decode, c)
     for k in range(1, chips):
-        add(3, x_forward, k)
+        add(4, x_forward, k)
     for k in range(chips):
-        add(4, x_ready, k)
-    when_early = (2, 3, 3, 4, 5, 6, 7, 8, 9)
-    when_late = (3, 3, 4, 5, 6, 7, 8, 9, 10)
+        add(5, x_ready, k)
+    when_early = (3, 3, 3, 4, 5, 6, 7, 8, 9)
+    when_late = (4, 4, 5, 6, 7, 8, 9, 10, 11)
     for r in range(half + 1):
         for n in range(len(sides(r))):
             add(when_early[r], one_side, g_early, r, n)
     for r in range(half - 1):
         add(when_late[r] + 1, on_sides, g_pass, r)
+        if r < half - 2:
+            add(when_late[r] + 2, on_sides, g_sum, r)
     for r in range(half + 1):
         for n in range(len(sides(r))):
             add(when_late[r], one_side, g_late, r, n)
     for q in range(half):
-        add((5, 5, 5, 6, 6, 7, 8, 9)[q], gw_pair, q, early)
+        add((6, 6, 6, 7, 7, 7, 8, 9)[q], gw_pair, q, early)
     for q in range(half):
-        add((5, 5, 6, 6, 7, 8, 9, 10)[q], gw_pair, q, late)
+        add((6, 6, 7, 7, 8, 9, 10, 11)[q], gw_pair, q, late)
+    shown = [(c, q) for c in early for q in range(groups // unroll)]
+    hidden = shown[:11]
+    for n, (c, q) in enumerate(hidden):
+        if q == 0:
+            add(9 if n < 5 else 10, scale_part, c)
+        add(9 if n < 5 else 10, piece, c, q)
     for at, job in todo:
         if at == 0:
             job()
@@ -340,12 +369,16 @@
     for at, job in todo:
         if at == last + 1:
             job()
-    for n, c in enumerate(early + late):
+    on_sides(g_pass, half - 1)
+    on_sides(g_sum, half - 2)
+    for c, q in shown[11:12]:
+        piece(c, q)
+    for n, c in enumerate(early[3:] + late):
         finish(c)
         if n == 0:
-            on_sides(g_pass, half - 1)
-        if n == 1:
-            g_pass(left_of(half), 2 * half - 1)
+            on_sides(g_pass, half)
+        if n == 2:
+            on_sides(g_sum, half - 1)
 
     def s_copy(k):
         dev = lax.rem(iz + k, nz)
@@ -374,6 +407,7 @@
     for k in range(1, nd):
         h_copy(k).start()
     hplane[jd] = hbk[mine]
+    on_sides(g_sum, half)
     for k in range(1, nd):
         src = lax.rem(jd + nd - k, nd)
         remote(hbk.at[0], hplane.at[src], hx_send.at[0], hx_recv.at[src], dout=src).wait_recv()
@@ -392,16 +426,11 @@
         remote(sown, sz.at[src], s_send.at[0], s_recv.at[src], din=src).wait_recv()
     scale_out[...] = jnp.sum(sz[...], axis=0)
 
-    for k in range(1, chips):
-        src = lax.rem(chip + chips - k, chips)
-        remote(rss.at[0], rsr.at[src], r_send.at[0], r_recv.at[src], dout=2 * src + core).wait_recv()
-    slot_own = 0
-    dist = lax.rem(chip - iz + nz, nz)
-    slot_own = jnp.where(dist == 0, 0, jnp.where(dist < half, 2 * dist, 2 * (nz - dist) - 1))
-    pltpu.make_async_copy(rss.at[slot_own], rsr.at[chip], r_send.at[slot_own]).wait()
-    acc = rsr[0].astype(f32)
-    for k in range(1, chips):
-        acc = acc + rsr[k].astype(f32)
+    acc = rsy[my_y].astype(f32)
+    for k in range(1, chips // across):
+        src = lax.rem(my_y + k, chips // across)
+        remote(rsy.at[0], rsr.at[src], y_send.at[0], y_recv.at[src], dout=mate).wait_recv()
+        acc = acc + rsr[src].astype(f32)
     gx_out[...] = acc.astype(bf16)
 
     for k in range(1, nz):
@@ -445,9 +474,16 @@
     for k in range(nz):
         remote(gst.at[k, 1 - core], gpr.at[k], p_send.at[k], p_recv.at[k], dout=mate).wait_send()
 
-        @pl.when(k != slot_own)
+        block = iz if k == 0 else (left_of((k + 1) // 2) if k % 2 else right_of(k // 2))
+
+        @pl.when(lax.rem(block, across) != my_x)
         def _():
-            remote(rss.at[k], rsr.at[chip], r_send.at[k], r_recv.at[chip], dout=mate).wait_send()
+            remote(rss.at[k], rsx.at[0, 0], r_send.at[k], r_recv.at[0, 0], dout=mate).wait_send()
+
+    for k in range(chips // across):
+        @pl.when(k != my_y)
+        def _():
+            remote(rsy.at[k], rsr.at[0], y_send.at[k], y_recv.at[0], dout=mate).wait_send()
 
 
 def fused(nz, nd, x, gy, codes, books, scales):
@@ -477,7 +513,9 @@
         V((nz, 2, rows // 2, feats), bf16),
         V((nz, rows // 2, feats), bf16),
         V((nz, rows // 2, feats), bf16),
-        V((chips, rows // 2, feats), bf16),
+        V((chips // 4, 4, rows // 2, feats), bf16),
+        V((chips // 4, rows // 2, feats), bf16),
+        V((chips // 4, rows // 2, feats), bf16),
         V((BOOKS, HIGH, LOW * 8), f32),
         V((8,) + tile, f32),
         V((nd,) + tile, f32),
@@ -493,7 +531,9 @@
         D((nz,)),
         D((nz,)),
         D((nz,)),
-        D((chips,)),
+        D((chips // 4, 4)),
+        D((chips // 4,)),
+        D((chips // 4,)),
         D((nd,)),
         D((nd,)),
         D((nz,)),

time: 93.3 us -> 97.8 us (1.048)
  Pallas kernels: 89 us -> 93.5 us
    pallas_call x1, Pallas kernels: 89 us -> 93.5 us  [fused(): pl.pallas_call(functools.partial(kernel, nz, nd), out_shape=(jax.ShapeDty...]
where the time goes in v4:
time: 97.8 us; the launch traced here: 97.5 us
  Pallas kernels  93.5 us (96%)
  other arithmetic  2 us (2%)
  local copies, waits for them, and re-layouts  1.34 us (1%)
    pallas_call x1, Pallas kernels, fused(): pl.pallas_call(functools.partial(kernel, nz, nd), out_shape=(jax.ShapeDty...  93.5 us
    sub x2, other arithmetic, adam_step(): return (param - adam_rate * update, mean_new, var_new)  2 us

profile of v4, /device:TPU:1, one launch (start us, length us, event | category | flops | bytes accessed | tf_op | source)
XLA Modules:
  0.0 97.5 jit_solution(2812507935086300905)
XLA Ops:
  0.6 0.0 copy-start.1
  0.6 0.0 copy-start.3
  0.7 0.0 copy-start.4
  0.7 93.5 %fused.1 = (bf16[64,512]{1,0:T(8,128)(2,1)}, f32[2,8,256]{2,1,0:T(8,128)}, f32[8,128]{1,0:T(8,128)}) custom-call(bf16[64,512]{1,0:T(8,128)(2,1)} %x_hbm.1, bf16[128,896]{1,0:T(8,128)(2,1)} %gy_hbm.1, s32[2,64,896]{2,1,0:T(8,128)} %codes_hbm.1, f32[2,8,256]{2,1,0:T(8,128)} %bitcast.18, f32[896]{0:T(1024)} %scales_hbm.1), custom_call_target="tpu_custom_call" | custom-call | tf_op jit(solution)/shard_map/fused/pallas_call | solution.py:546
  94.1 0.0 copy-done.1
  94.2 0.0 copy-done.3
  94.2 0.0 copy-done.4
  94.2 0.0 copy-start.6
  94.2 0.0 copy-start.7
  94.2 0.0 copy-start
  94.2 1.4 %multiply_subtract_fusion = (f32[2,256,8]{1,2,0:T(8,128)}, f32[2,256,8]{1,2,0:T(8,128)}, f32[2,256,8]{1,2,0:T(8,128)}, f32[2,256,8]{1,2,0:T(8,128)}) fusion(f32[2,256,8]{1,2,0:T(8,128)S(1)} %copy-done.1, f32[2,8,256]{2,1,0:T(8,128)} %get-tuple-element.12, f32[2,256,8]{1,2,0:T(8,128)S(1)} %copy-done.3, f32[2,256,8]{1,2,0:T(8,128)S(1)} %copy-done.4), kind=kLoop, calls=%fused_computation.3 | loop fusion | flops 57344 | bytes 131072 | tf_op jit(solution)/shard_map/sub | solution.py:36
  95.6 0.0 copy-start.5
  95.6 0.0 copy-start.2
  95.6 0.0 copy-done.6
  95.6 0.0 copy-done.7
  95.6 0.7 copy-done.5
  96.3 0.0 copy-done.2
  96.3 0.6 multiply_subtract_fusion.1
  96.9 0.0 copy-done
  96.9 0.6 copy.18
Async XLA Ops:
  0.6 93.5 %copy-start.1 = (f32[2,256,8]{1,2,0:T(8,128)S(1)}, f32[2,256,8]{1,2,0:T(8,128)}, u32[]{:S(2)}) copy-start(f32[2,256,8]{1,2,0:T(8,128)} %param.12) | copy-start | bytes 49156
  0.6 93.5 %copy-start.3 = (f32[2,256,8]{1,2,0:T(8,128)S(1)}, f32[2,256,8]{1,2,0:T(8,128)}, u32[]{:S(2)}) copy-start(f32[2,256,8]{1,2,0:T(8,128)} %param.14) | copy-start | bytes 49156
  0.7 93.5 %copy-start.4 = (f32[2,256,8]{1,2,0:T(8,128)S(1)}, f32[2,256,8]{1,2,0:T(8,128)}, u32[]{:S(2)}) copy-start(f32[2,256,8]{1,2,0:T(8,128)} %param.15) | copy-start | bytes 49156
  94.2 1.4 %copy-start.6 = (f32[896]{0:T(1024)S(1)}, f32[896]{0:T(1024)}, u32[]{:S(2)}) copy-start(f32[896]{0:T(1024)} %param.17) | copy-start | bytes 10756
  94.2 1.4 %copy-start.7 = (f32[8,128]{1,0:T(8,128)S(1)}, f32[8,128]{1,0:T(8,128)}, u32[]{:S(2)}) copy-start(f32[8,128]{1,0:T(8,128)} %get-tuple-element.13) | copy-start | bytes 12292
  94.2 2.7 %copy-start = (bf16[64,512]{1,0:T(8,128)(2,1)S(1)}, bf16[64,512]{1,0:T(8,128)(2,1)}, u32[]{:S(2)}) copy-start(bf16[64,512]{1,0:T(8,128)(2,1)} %get-tuple-element.29) | copy-start | bytes 196612
  95.6 0.7 copy-start.5
  95.6 0.7 copy-start.2

commit v5 on v3

--- a/solution.py
+++ b/solution.py
@@ -321,6 +321,10 @@
         add((5, 5, 5, 6, 6, 7, 8, 9)[q], gw_pair, q, early)
     for q in range(half):
         add((5, 5, 6, 6, 7, 8, 9, 10)[q], gw_pair, q, late)
+    hidden = min(3, groups // unroll)
+    add(9, scale_part, early[0])
+    for q in range(hidden):
+        add(9, piece, early[0], q)
     for at, job in todo:
         if at == 0:
             job()
@@ -341,10 +345,14 @@
         if at == last + 1:
             job()
     for n, c in enumerate(early + late):
-        finish(c)
         if n == 0:
+            for q in range(hidden, groups // unroll):
+                piece(c, q)
+        else:
+            finish(c)
+        if n == 1:
             on_sides(g_pass, half - 1)
-        if n == 1:
+        if n == 2:
             g_pass(left_of(half), 2 * half - 1)
 
     def s_copy(k):

time: 93.3 us -> 93.2 us (level)
  no operation moved by 1% of the time
where the time goes in v5:
time: 93.2 us; the launch traced here: 93 us
  Pallas kernels  88.9 us (95%)
  other arithmetic  2 us (2%)
  local copies, waits for them, and re-layouts  1.34 us (1%)
    pallas_call x1, Pallas kernels, fused(): pl.pallas_call(functools.partial(kernel, nz, nd), out_shape=(jax.ShapeDty...  88.9 us
    sub x2, other arithmetic, adam_step(): return (param - adam_rate * update, mean_new, var_new)  2 us

profile of v5, /device:TPU:1, one launch (start us, length us, event | category | flops | bytes accessed | tf_op | source)
XLA Modules:
  0.0 93.0 jit_solution(4294780268900047829)
XLA Ops:
  0.6 0.0 copy-start.1
  0.6 0.0 copy-start.3
  0.7 0.0 copy-start.4
  0.7 88.9 %fused.1 = (bf16[64,512]{1,0:T(8,128)(2,1)}, f32[2,8,256]{2,1,0:T(8,128)}, f32[8,128]{1,0:T(8,128)}) custom-call(bf16[64,512]{1,0:T(8,128)(2,1)} %x_hbm.1, bf16[128,896]{1,0:T(8,128)(2,1)} %gy_hbm.1, s32[2,64,896]{2,1,0:T(8,128)} %codes_hbm.1, f32[2,8,256]{2,1,0:T(8,128)} %bitcast.18, f32[896]{0:T(1024)} %scales_hbm.1), custom_call_target="tpu_custom_call" | custom-call | tf_op jit(solution)/shard_map/fused/pallas_call | solution.py:514
  89.6 0.0 copy-done.1
  89.6 0.0 copy-done.3
  89.6 0.0 copy-done.4
  89.6 0.0 copy-start.6
  89.6 0.0 copy-start.7
  89.6 0.0 copy-start
  89.6 1.4 %multiply_subtract_fusion = (f32[2,256,8]{1,2,0:T(8,128)}, f32[2,256,8]{1,2,0:T(8,128)}, f32[2,256,8]{1,2,0:T(8,128)}, f32[2,256,8]{1,2,0:T(8,128)}) fusion(f32[2,256,8]{1,2,0:T(8,128)S(1)} %copy-done.1, f32[2,8,256]{2,1,0:T(8,128)} %get-tuple-element.12, f32[2,256,8]{1,2,0:T(8,128)S(1)} %copy-done.3, f32[2,256,8]{1,2,0:T(8,128)S(1)} %copy-done.4), kind=kLoop, calls=%fused_computation.3 | loop fusion | flops 57344 | bytes 131072 | tf_op jit(solution)/shard_map/sub | solution.py:36
  91.0 0.0 copy-start.5
  91.0 0.0 copy-start.2
  91.0 0.0 copy-done.6
  91.0 0.0 copy-done.7
  91.0 0.7 copy-done.5
  91.7 0.0 copy-done.2
  91.7 0.6 multiply_subtract_fusion.1
  92.3 0.0 copy-done
  92.3 0.6 copy.18
Async XLA Ops:
  0.6 88.9 %copy-start.1 = (f32[2,256,8]{1,2,0:T(8,128)S(1)}, f32[2,256,8]{1,2,0:T(8,128)}, u32[]{:S(2)}) copy-start(f32[2,256,8]{1,2,0:T(8,128)} %param.12) | copy-start | bytes 49156
  0.6 88.9 %copy-start.3 = (f32[2,256,8]{1,2,0:T(8,128)S(1)}, f32[2,256,8]{1,2,0:T(8,128)}, u32[]{:S(2)}) copy-start(f32[2,256,8]{1,2,0:T(8,128)} %param.14) | copy-start | bytes 49156
  0.7 88.9 %copy-start.4 = (f32[2,256,8]{1,2,0:T(8,128)S(1)}, f32[2,256,8]{1,2,0:T(8,128)}, u32[]{:S(2)}) copy-start(f32[2,256,8]{1,2,0:T(8,128)} %param.15) | copy-start | bytes 49156
  89.6 1.4 %copy-start.6 = (f32[896]{0:T(1024)S(1)}, f32[896]{0:T(1024)}, u32[]{:S(2)}) copy-start(f32[896]{0:T(1024)} %param.17) | copy-start | bytes 10756
  89.6 1.4 %copy-start.7 = (f32[8,128]{1,0:T(8,128)S(1)}, f32[8,128]{1,0:T(8,128)}, u32[]{:S(2)}) copy-start(f32[8,128]{1,0:T(8,128)} %get-tuple-element.13) | copy-start | bytes 12292
  89.6 2.7 %copy-start = (bf16[64,512]{1,0:T(8,128)(2,1)S(1)}, bf16[64,512]{1,0:T(8,128)(2,1)}, u32[]{:S(2)}) copy-start(bf16[64,512]{1,0:T(8,128)(2,1)} %get-tuple-element.29) | copy-start | bytes 196612
  91.0 0.7 copy-start.5
  91.0 0.7 copy-start.2
